TPU v7x, 512 devices: a whole 4x8x8 slice. The times are simulated.
512 devices in a mesh: grid: 32 (over y_lo, z, core), occ: 16 (over x, y_hi).
Axes of the slice: x: 4, y: 8 (y_hi: 4, y_lo: 2; y = y_hi * 2 + y_lo), z: 8, core: 2. Of those that a mesh axis runs over, the one named last changes fastest.
Arguments:
- orbital_values: bfloat16 [8192, 16000], P('grid', 'occ'), may hold values from -6 to 6
- occupied: bfloat16 [16000, 512], P('occ', 'grid'), may hold values from -0.046875 to 0.046875
- trial: bfloat16 [16000, 512], P('occ', 'grid'), may hold values from -0.046875 to 0.046875
- point_weights: float32 [8192], P('grid'), may hold values from 0.1 to 1
- batch_sizes: int32 [256], P('grid'), may hold values from 1 to 32, 4096 in all
- significant: int32 [256, 128], P('grid', 'occ'), may hold values 0 or 1
Outputs:
- exchange: float32 [16000, 512], P('occ', 'grid')
Inputs may be any that keep to these rules, and one draw needn't show every extreme that they name: `batch_sizes`: batch sizes sum to 4096 and the largest is exactly 32.
All inputs are finite; a program needn't handle non-finite values. No bound on the sum of `batch_sizes` or of `significant` on one device may be relied on, other than what follows from the above.
Results may differ from a plain program's by a relative error of at most 0.0027.
Values may be sent and summed in bfloat16 or wider, within the bound.
A program may use at most 64 MiB of HBM per device.

v0:
```python
import math

import jax
import jax.numpy as jnp
from jax import lax
from jax.sharding import PartitionSpec as P


def screen(values, sizes, significant):
    rows, cols = values.shape
    batches = sizes.shape[0]
    blocks = significant.shape[1]
    blocked = (
        values.reshape(batches, rows // batches, blocks, cols // blocks)
        * significant.astype(values.dtype)[:, None, :, None]
    )
    position = lax.broadcasted_iota(jnp.int32, (batches, rows // batches), 1)
    live = (position < sizes[:, None]).astype(jnp.float32).reshape(rows)
    return (blocked.reshape(rows, cols), live)


def per_device(orbital_values, occupied, trial, point_weights, batch_sizes, significant):
    screened, live = screen(orbital_values, batch_sizes, significant)
    rows = screened.shape[0]
    grid_count = lax.axis_size("grid")
    columns = occupied.shape[1]
    total = columns * grid_count
    joined = jnp.concatenate((occupied, trial), axis=1)
    panels_all = lax.all_gather(joined, "grid", axis=1, tiled=True)
    terms = jnp.dot(screened, panels_all, preferred_element_type=jnp.float32)
    stacked = (
        terms.reshape(rows, grid_count, 2, columns).transpose(0, 2, 1, 3).reshape(rows, 2, total)
    )
    weight = point_weights * live
    occ_scale = 1.0 / math.sqrt(total)
    shares = lax.psum_scatter(stacked, "occ", scatter_dimension=2, tiled=True)
    orbitals = shares[:, 0]
    response = shares[:, 1]
    density = lax.psum(jnp.sum(orbitals * response, axis=1), "occ") * occ_scale
    kernel = (weight[:, None] * (density[:, None] * orbitals + response)).astype(jnp.bfloat16)
    kernel_all = lax.all_gather(kernel, "occ", axis=1, tiled=True)
    partial_value = lax.dot_general(
        screened, kernel_all, (((0,), (0,)), ((), ())), preferred_element_type=jnp.float32
    )
    npoints = rows * grid_count
    return lax.psum_scatter(partial_value, "grid", scatter_dimension=1, tiled=True) / math.sqrt(
        npoints
    )


def solution(mesh):
    placed = (
        P("grid", "occ"),
        P("occ", "grid"),
        P("occ", "grid"),
        P("grid"),
        P("grid"),
        P("grid", "occ"),
    )
    return jax.shard_map(
        per_device, mesh=mesh, in_specs=placed, out_specs=P("occ", "grid"), check_vma=False
    )
```

profile of v0, /device:TPU:1, one launch (start us, length us, event | category | flops | bytes accessed | tf_op | source)
XLA Modules:
  0.0 389.3 jit_solution(2788873274233231226)
XLA Ops:
  6.5 0.0 copy-start
  6.5 0.0 all-gather.2.cloned.1.call-start
  6.5 1.5 pad_maximum_fusion
  8.0 0.0 all-gather.2.cloned.1.call-update
  8.0 0.0 reduce-scatter.3.cloned.1.call-start
  8.1 0.7 convert_element_type.8
  8.8 0.1 mul.39
  8.9 0.4 mul.40
  9.3 0.0 copy-done
  9.3 0.2 copy.8
  9.6 0.2 mul.41
  9.8 73.2 %all-gather.2.cloned.1.call-done = bf16[1000,1024]{0,1:T(8,128)(2,1)} async-done(((bf16[1000,32]{0,1:T(8,128)(2,1)}), bf16[1000,1024]{0,1:T(8,128)(2,1)}) %all-gather.2.cloned.1.call-update) | async-done | bytes 2048016 | tf_op jit(solution)/shard_map/all_gather | solution.py:29
  82.9 3.1 fusion.2
  86.0 0.0 copy-start.2
  86.0 0.0 copy-start.1
  86.0 1.6 copy.11
  87.6 0.0 reduce-scatter.3.cloned.1.call-update
  87.7 0.0 reduce-scatter.5.cloned.1.call-start
  87.7 0.0 copy-done.2
  87.7 0.1 iota_compare_fusion
  87.8 0.1 lt.14
  87.9 0.0 copy-done.1
  87.9 89.5 %reduce-scatter.3.cloned.1.call-done = f32[256,2,32]{0,2,1:T(8,128)} async-done(((f32[256,2,512]{0,2,1:T(8,128)}), f32[256,2,32]{0,2,1:T(8,128)}) %reduce-scatter.3.cloned.1.call-update) | async-done | bytes 65552 | tf_op jit(solution)/shard_map/reduce_scatter | solution.py:36
  177.4 0.8 multiply_reduce_fusion
  178.2 35.5 %psum.7 = f32[256]{0:T(256)S(1)} all-reduce(f32[256]{0:T(256)S(1)} %multiply_reduce_fusion), channel_id=1, replica_groups=mesh['grid'=32,'occ'=16] {'occ'}, use_global_device_ids=true, to_apply=%region_2.0 | all-reduce | flops 256 | bytes 2048 | tf_op jit(solution)/shard_map/psum | solution.py:39
  213.8 0.8 multiply_convert_fusion
  214.5 32.8 %all_gather.7 = bf16[256,512]{0,1:T(8,128)(2,1)S(1)} all-gather(bf16[256,32]{0,1:T(8,128)(2,1)S(1)} %multiply_convert_fusion), channel_id=1, replica_groups=mesh['grid'=32,'occ'=16] {'occ'}, dimensions={1}, use_global_device_ids=true | all-gather | bytes 278528 | tf_op jit(solution)/shard_map/all_gather | solution.py:41
  247.4 1.8 fusion.6
  249.2 0.0 reduce-scatter.5.cloned.1.call-update
  249.2 132.1 %reduce-scatter.5.cloned.1.call-done = f32[1000,16]{0,1:T(8,128)} async-done(((f32[1000,512]{0,1:T(8,128)}), f32[1000,16]{0,1:T(8,128)}) %reduce-scatter.5.cloned.1.call-update) | async-done | bytes 64016 | tf_op jit(solution)/shard_map/reduce_scatter | solution.py:46
  381.3 1.5 broadcast_multiply_fusion
  (2 shorter events, 0.0 us)
Async XLA Ops:
  6.5 2.8 copy-start
  6.5 76.4 %all-gather.2.cloned.1.call-start = ((), (), s32[]{:S(2)}) async-start(), calls=%async_computation.2 | async-start | bytes 2162688 | tf_op jit(solution)/shard_map/all_gather | solution.py:29
  8.0 169.4 %reduce-scatter.3.cloned.1.call-start = ((), (), s32[]{:S(2)}) async-start(), calls=%async_computation.3 | async-start | bytes 1114112 | tf_op jit(solution)/shard_map/reduce_scatter | solution.py:36
  86.0 1.7 copy-start.2
  86.0 1.9 copy-start.1
  87.7 293.6 %reduce-scatter.5.cloned.1.call-start = ((), (), s32[]{:S(2)}) async-start(), calls=%async_computation.4 | async-start | bytes 2162688 | tf_op jit(solution)/shard_map/reduce_scatter | solution.py:46
Sparse Core Ops, SparseCore 0:
  9.5 73.3 all-gather.1
  87.8 89.6 reduce-scatter.2
  249.3 131.8 reduce-scatter.4
where the time goes:
time: 393 us; the launch traced here: 389 us
  waiting for transfers between devices  295 us (75%)
  blocking collectives  68.4 us (17%)
  between operations  13.2 us (3%)
  other arithmetic  5.49 us (1%)
  matrix products  4.87 us (1%)
    reduce_scatter x1, waiting for transfers between devices, per_device(): lax.psum_scatter(partial_value, 'grid', scatter_dimension=1, tiled=True)  132 us
    reduce_scatter x1, waiting for transfers between devices, per_device(): shares = lax.psum_scatter(stacked, 'occ', scatter_dimension=2, tiled=True)  89.5 us
    all_gather x1, waiting for transfers between devices, per_device(): panels_all = lax.all_gather(joined, 'grid', axis=1, tiled=True)  73.2 us
    psum x1, blocking collectives, per_device(): density = lax.psum(jnp.sum(orbitals * response, axis=1), 'occ') * occ_scale  35.5 us
    all_gather x1, blocking collectives, per_device(): kernel_all = lax.all_gather(kernel, 'occ', axis=1, tiled=True)  32.8 us
  transfers between devices with their start and end apart: 3, of which 3 were waited for; matrix products, arithmetic and copies ran while one was open for 0% of the time, Pallas kernels for 0%

commit v1 on v0

v1 whole, which is shorter than its diff:
```python
import functools
import math

import jax
import jax.numpy as jnp
from jax import lax
from jax.experimental import pallas as pl
from jax.experimental.pallas import tpu as pltpu
from jax.sharding import PartitionSpec as P

MESH = pl.DeviceIdType.MESH
NX, NYH, NYL, NZ, NC = 4, 4, 2, 8, 2
CAP = 32

SETS = (
    ((0, 0), (1, 0), (0, 1), (0, 7)),
    ((0, 2), (0, 6), (1, 1), (1, 7)),
    ((0, 3), (0, 5), (1, 2), (1, 6)),
    ((0, 4), (1, 3), (1, 5), (1, 4)),
)
WHERE = {slot: (s, i) for s, row in enumerate(SETS) for i, slot in enumerate(row)}


def kernel(
    v_ref, occ_ref, tri_ref, w_ref, sz_ref, sig_ref, out_ref,
    panels, vraw, sigp, smat, prod,
    x1p, x1m, x3p, x3m, a5p, a5m, x5p, x5m,
    turned, yrecv, dens_out, dens_in, kall,
    xsend, xrecv, zsend, zrecv,
    sems, p_sems, c_sems, x_sems, y_sems, k_sems, d_sems,
):
    g, o = lax.axis_index("grid"), lax.axis_index("occ")
    yl, z, c = g // (NZ * NC), (g // NC) % NZ, g % NC
    x, yh = o // NYH, o % NYH
    nrow = occ_ref.shape[0]
    npt = v_ref.shape[1]

    def grid_at(dy, dz, dc):
        return (((yl + dy) % NYL) * NZ + (z + dz) % NZ) * NC + (c + dc) % NC

    def occ_at(dx, dyh):
        return ((x + dx) % NX) * NYH + (yh + dyh) % NYH

    sent = []

    def send(src, dst, recv_sem, dy=0, dz=0, dc=0, dx=0, dyh=0):
        copy = pltpu.make_async_remote_copy(
            src_ref=src, dst_ref=dst, send_sem=sems.at[len(sent)], recv_sem=recv_sem,
            device_id={"grid": grid_at(dy, dz, dc), "occ": occ_at(dx, dyh)}, device_id_type=MESH,
        )
        copy.start()
        sent.append(copy)

    def arrive(dst, recv_sem):
        pltpu.make_async_remote_copy(
            src_ref=dst, dst_ref=dst, send_sem=sems.at[0], recv_sem=recv_sem,
            device_id={"grid": grid_at(0, 0, 1), "occ": o}, device_id_type=MESH,
        ).wait_recv()

    barrier = pltpu.get_barrier_semaphore()
    peers = (
        dict(dc=1), dict(dy=1), dict(dz=1), dict(dz=7), dict(dx=1), dict(dx=3),
        dict(dyh=1), dict(dyh=2), dict(dyh=3),
    )
    for peer in peers:
        pl.semaphore_signal(
            barrier, inc=1,
            device_id={
                "grid": grid_at(peer.get("dy", 0), peer.get("dz", 0), peer.get("dc", 0)),
                "occ": occ_at(peer.get("dx", 0), peer.get("dyh", 0)),
            },
            device_id_type=MESH,
        )
    pl.semaphore_wait(barrier, len(peers))

    def place(slot, t):
        s, i = WHERE[slot]
        return panels.at[s, t, i]

    def p_sem(slot, t):
        s, i = WHERE[slot]
        return p_sems.at[(s * 4 + i) * 2 + t]

    own = (occ_ref, tri_ref)
    for t in range(2):
        send(own[t], place((0, 7), t), p_sem((0, 7), t), dz=1)
        send(own[t], place((0, 1), t), p_sem((0, 1), t), dz=7)
        send(own[t], place((1, 0), t), p_sem((1, 0), t), dy=1)
    send(sig_ref, sigp, c_sems.at[0], dc=1)
    send(v_ref, vraw, c_sems.at[1], dc=1)
    for t in range(2):
        panels[0, t, 0] = own[t][...]

    def got(slot, t):
        arrive(place(slot, t), p_sem(slot, t))

    def relay(slot, t, moves):
        got(slot, t)
        for to, step in moves:
            send(place(slot, t), place(to, t), p_sem(to, t), **step)

    up, down, over = dict(dz=1), dict(dz=7), dict(dy=1)

    nblock, nbatch = sig_ref.shape[1], sig_ref.shape[0]
    width = v_ref.shape[0] // nblock

    def screen(values, significant):
        sig = significant.astype(jnp.float32).astype(jnp.bfloat16)
        eye = (
            lax.broadcasted_iota(jnp.int32, (nblock, nblock), 0)
            == lax.broadcasted_iota(jnp.int32, (nblock, nblock), 1)
        ).astype(jnp.bfloat16)
        flipped = lax.dot_general(
            eye, sig, (((1,), (1,)), ((), ())), preferred_element_type=jnp.float32
        ).astype(jnp.bfloat16)
        spread = (
            lax.broadcasted_iota(jnp.int32, (nbatch, npt), 1) // CAP
            == lax.broadcasted_iota(jnp.int32, (nbatch, npt), 0)
        ).astype(jnp.bfloat16)
        lanes = jnp.dot(flipped, spread, preferred_element_type=jnp.float32).astype(jnp.bfloat16)
        rows = (
            lax.broadcasted_iota(jnp.int32, (v_ref.shape[0], nblock), 0) // width
            == lax.broadcasted_iota(jnp.int32, (v_ref.shape[0], nblock), 1)
        ).astype(jnp.bfloat16)
        mask = jnp.dot(rows, lanes, preferred_element_type=jnp.float32)
        return values * mask.astype(jnp.bfloat16)

    smat[c] = screen(v_ref[...], sig_ref[...])

    for t in range(2):
        relay((1, 0), t, (((1, 7), up), ((1, 1), down)))
        relay((0, 7), t, (((0, 6), up),))
        relay((0, 1), t, (((0, 2), down),))
    arrive(sigp, c_sems.at[0])
    arrive(vraw, c_sems.at[1])
    smat[1 - c] = screen(vraw[...], sigp[...])

    half = nrow * 4

    def multiply(s):
        lhs = panels[s].reshape(2 * half, v_ref.shape[0])
        for k in range(NC):
            res = jnp.dot(lhs, smat[k], preferred_element_type=jnp.float32)
            for h in range(2):
                prod[s, 2 * k + h] = res[:, h * 128 : (h + 1) * 128]

    lo, hi = pl.ds(0, half), pl.ds(half, half)

    def x_first(s):
        across = prod.at[s, (x + 2) % NX]
        send(across.at[lo], x1p.at[s], x_sems.at[s, 0], dx=1)
        send(across.at[hi], x1m.at[s], x_sems.at[s, 1], dx=3)
        send(prod.at[s, (x + 1) % NX].at[hi], x3p.at[s], x_sems.at[s, 2], dx=1)
        send(prod.at[s, (x + 3) % NX].at[lo], x3m.at[s], x_sems.at[s, 3], dx=3)

    def x_second(s):
        arrive(x1p.at[s], x_sems.at[s, 0])
        a5p[s] = x1p[s] + prod[s, (x + 1) % NX, :half]
        send(a5p.at[s], x5p.at[s], x_sems.at[s, 4], dx=1)
        arrive(x1m.at[s], x_sems.at[s, 1])
        a5m[s] = x1m[s] + prod[s, (x + 3) % NX, half:]
        send(a5m.at[s], x5m.at[s], x_sems.at[s, 5], dx=3)

    def x_last(s):
        arrive(x3p.at[s], x_sems.at[s, 2])
        arrive(x3m.at[s], x_sems.at[s, 3])
        arrive(x5p.at[s], x_sems.at[s, 4])
        arrive(x5m.at[s], x_sems.at[s, 5])
        top = prod[s, x, :half] + x3m[s] + x5p[s]
        low = prod[s, x, half:] + x3p[s] + x5m[s]
        both = jnp.concatenate((top, low), axis=0)
        turned[s] = both.T.reshape(NYH, CAP, 2 * half)
        for k in range(1, NYH):
            send(turned.at[s, (yh + k) % NYH], yrecv.at[s, k - 1], y_sems.at[s, k - 1], dyh=k)

    multiply(0)
    x_first(0)
    for t in range(2):
        relay((0, 6), t, (((0, 5), up),))
        relay((0, 2), t, (((0, 3), down),))
        relay((1, 7), t, (((1, 6), up),))
        relay((1, 1), t, (((1, 2), down),))
    x_second(0)
    multiply(1)
    x_first(1)
    for t in range(2):
        relay((0, 5), t, ((((0, 4), up),) if t == 0 else ()) + (((1, 5), over),))
        relay((0, 3), t, ((((0, 4), down),) if t == 1 else ()) + (((1, 3), over),))
    x_last(0)
    x_second(1)
    for t in range(2):
        got((1, 6), t)
        got((1, 2), t)
    multiply(2)
    x_first(2)
    for t in range(2):
        relay((0, 4), t, (((1, 4), over),))
    x_last(1)
    x_second(2)
    for t in range(2):
        got((1, 5), t)
        got((1, 3), t)
        got((1, 4), t)
    multiply(3)
    x_first(3)
    x_last(2)
    x_second(3)
    x_last(3)

    lane = lax.broadcasted_iota(jnp.int32, (CAP, 2 * half), 1)
    units, rolled = [], []
    part = jnp.zeros((CAP, 1), jnp.float32)
    for s in range(4):
        for k in range(1, NYH):
            arrive(yrecv.at[s, k - 1], y_sems.at[s, k - 1])
        unit = turned[s, yh] + yrecv[s, 0] + yrecv[s, 1] + yrecv[s, 2]
        other = pltpu.roll(unit, half, 1)
        units.append(unit)
        rolled.append(other)
        part += jnp.sum(jnp.where(lane < half, unit * other, 0.0), axis=1, keepdims=True)

    batch = o % nbatch
    row_of = lax.broadcasted_iota(jnp.int32, (CAP, npt), 0)
    lane_of = lax.broadcasted_iota(jnp.int32, (CAP, npt), 1)
    weight = jnp.sum(
        jnp.where(lane_of == row_of + batch * CAP, w_ref[...], 0.0), axis=1, keepdims=True
    )
    count = jnp.sum(
        jnp.where(
            lax.broadcasted_iota(jnp.int32, (1, nbatch), 1) == batch,
            sz_ref[...].astype(jnp.float32), 0.0,
        ),
        axis=1, keepdims=True,
    )
    live = lax.broadcasted_iota(jnp.int32, (CAP, 1), 0).astype(jnp.float32) < count
    weight = jnp.where(live, weight, 0.0)
    dens_out[...] = jnp.where(lane < half, part, weight)
    send(dens_out, dens_in, d_sems.at[0], dc=1)
    arrive(dens_in, d_sems.at[0])
    total = 2 * nrow * NYL * NZ
    density = (part + dens_in[:, 0:1]) * (1.0 / math.sqrt(total))
    weight = jnp.where(o // nbatch == c, weight, dens_in[:, half : half + 1])
    for p in range(2):
        a, b = 2 * p, 2 * p + 1
        value = jnp.where(
            lane < half, density * units[a] + rolled[a], density * rolled[b] + units[b]
        )
        kall[o, :, p * 128 : (p + 1) * 128] = (weight * value).astype(jnp.bfloat16)

    def k_from(dx, dyh):
        return kall.at[occ_at(dx, dyh)]

    for k in range(1, NYH):
        send(k_from(0, 0), k_from(0, 0), k_sems.at[(NYH - k) % NYH], dyh=k)
    for k in (0, 1, 3, 2):
        if k:
            arrive(k_from(0, k), k_sems.at[k])
        for d in (1, 3, 2):
            send(k_from(0, k), k_from(0, k), k_sems.at[((NX - d) % NX) * NYH + k], dx=d)
    for d in (1, 3, 2):
        for k in (0, 1, 3, 2):
            arrive(k_from(d, k), k_sems.at[d * NYH + k])

    kt = [
        kall[k * nbatch : (k + 1) * nbatch].reshape(npt, 4 * half).T for k in range(NC)
    ]

    ys = [(dz, WHERE[(1, dz)]) for dz in range(NZ)]
    held = {}
    for s in (3, 2, 1, 0):
        res = sum(
            lax.dot_general(
                kt[k][s * half : (s + 1) * half], smat[k], (((1,), (1,)), ((), ())),
                preferred_element_type=jnp.float32,
            )
            for k in range(NC)
        )
        for i, (dy, dz) in enumerate(SETS[s]):
            block = res[i * nrow : (i + 1) * nrow]
            if dy:
                xsend[dz] = block.astype(jnp.bfloat16)
                send(xsend.at[dz], xrecv.at[dz], d_sems.at[1 + dz], dy=1)
            else:
                held[dz] = block
    mine = None
    for dz in (4, 3, 5, 2, 6, 1, 7, 0):
        arrive(xrecv.at[dz], d_sems.at[1 + dz])
        value = held[dz] + xrecv[dz].astype(jnp.float32)
        if dz:
            zsend[dz - 1] = value.astype(jnp.bfloat16)
            send(zsend.at[dz - 1], zrecv.at[dz - 1], d_sems.at[8 + dz], dz=dz)
        else:
            mine = value
    for dz in (1, 7, 2, 6, 3, 5, 4):
        arrive(zrecv.at[dz - 1], d_sems.at[8 + dz])
        mine = mine + zrecv[dz - 1].astype(jnp.float32)
    points = npt * NYL * NZ * NC
    out_ref[...] = mine * (1.0 / math.sqrt(points))
    for copy in sent:
        copy.wait_send()


def per_device(orbital_values, occupied, trial, point_weights, batch_sizes, significant):
    v, occ, tri = orbital_values.T, occupied.T, trial.T
    m, npt = v.shape
    nrow = occ.shape[0]
    half = 4 * nrow
    f32, bf16 = jnp.float32, jnp.bfloat16
    dma = pltpu.SemaphoreType.DMA
    out = pl.pallas_call(
        kernel,
        out_shape=jax.ShapeDtypeStruct((nrow, m), f32),
        in_specs=[pl.BlockSpec(memory_space=pltpu.VMEM)] * 6,
        out_specs=pl.BlockSpec(memory_space=pltpu.VMEM),
        scratch_shapes=[
            pltpu.VMEM((4, 2, 4, nrow, m), bf16),
            pltpu.VMEM((m, npt), bf16),
            pltpu.VMEM(significant.shape, jnp.int32),
            pltpu.VMEM((NC, m, npt), bf16),
            pltpu.VMEM((4, NX, 2 * half, 128), f32),
        ]
        + [pltpu.VMEM((4, half, 128), f32)] * 8
        + [
            pltpu.VMEM((4, NYH, CAP, 2 * half), f32),
            pltpu.VMEM((4, NYH - 1, CAP, 2 * half), f32),
            pltpu.VMEM((CAP, 2 * half), f32),
            pltpu.VMEM((CAP, 2 * half), f32),
            pltpu.VMEM((NX * NYH, CAP, 4 * half), bf16),
            pltpu.VMEM((NZ, nrow, m), bf16),
            pltpu.VMEM((NZ, nrow, m), bf16),
            pltpu.VMEM((NZ - 1, nrow, m), bf16),
            pltpu.VMEM((NZ - 1, nrow, m), bf16),
            dma((128,)),
            dma((32,)),
            dma((2,)),
            dma((4, 6)),
            dma((4, NYH - 1)),
            dma((NX * NYH,)),
            dma((1 + 8 + 8,)),
        ],
        compiler_params=pltpu.CompilerParams(
            collective_id=0, has_side_effects=True, vmem_limit_bytes=48 << 20
        ),
    )(v, occ, tri, point_weights.reshape(1, -1), batch_sizes.reshape(1, -1), significant)
    return out.T


def solution(mesh):
    placed = (
        P("grid", "occ"),
        P("occ", "grid"),
        P("occ", "grid"),
        P("grid"),
        P("grid"),
        P("grid", "occ"),
    )
    return jax.shard_map(
        per_device, mesh=mesh, in_specs=placed, out_specs=P("occ", "grid"), check_vma=False
    )
```

time: 393 us -> 70.9 us (0.18)
  waiting for transfers between devices: 295 us -> 0 us
  blocking collectives: 68.4 us -> 0 us
  Pallas kernels: 0 us -> 65.7 us
  between operations: 13.2 us -> 0.02 us
  other arithmetic: 5.49 us -> 0 us
  matrix products: 4.87 us -> 0 us
    reduce_scatter x2 -> x0, waiting for transfers between devices: 222 us -> none  [the longest x1 132 us: per_device(): lax.psum_scatter(partial_value, 'grid', scatter_dimension=1, tiled=True)]
    all_gather x1 -> x0, waiting for transfers between devices: 73.2 us -> none  [per_device(): panels_all = lax.all_gather(joined, 'grid', axis=1, tiled=True)]
    pallas_call x0 -> x1, Pallas kernels: none -> 65.7 us  [per_device(): pl.pallas_call(kernel, out_shape=jax.ShapeDtypeStruct((nrow, m), f32), in...]
    psum x1 -> x0, blocking collectives: 35.5 us -> none  [per_device(): density = lax.psum(jnp.sum(orbitals * response, axis=1), 'occ') * occ_scale]
    all_gather x1 -> x0, blocking collectives: 32.8 us -> none  [per_device(): kernel_all = lax.all_gather(kernel, 'occ', axis=1, tiled=True)]
    dot_general x2 -> x0, matrix products: 4.87 us -> none  [the longest x1 3.09 us: per_device(): terms = jnp.dot(screened, panels_all, preferred_element_type=jnp.float32)]
  transfers between devices with their start and end apart: 3 -> 0, of which waited for: 3 -> 0; matrix products, arithmetic and copies ran while one was open for 0% -> 0% of each run, Pallas kernels for 0% -> 0%
where the time goes in v1:
time: 70.9 us; the launch traced here: 69.6 us
  Pallas kernels  65.7 us (93%)
  local copies, waits for them, and re-layouts  3.88 us (5%)
    pallas_call x1, Pallas kernels, per_device(): pl.pallas_call(kernel, out_shape=jax.ShapeDtypeStruct((nrow, m), f32), in...  65.7 us
    unnamed x13, local copies, waits for them, and re-layouts  3.88 us

profile of v1, /device:TPU:1, one launch (start us, length us, event | category | flops | bytes accessed | tf_op | source)
XLA Modules:
  0.0 69.6 jit_solution(2265619735239633005)
XLA Ops:
  0.0 0.0 copy-start.3
  0.0 0.0 copy-start.4
  0.0 0.0 copy-start.5
  0.0 0.7 copy-done.3
  0.7 0.0 copy-done.4
  0.7 0.0 copy-done.5
  0.7 0.0 copy-start
  0.7 1.0 %copy-done = bf16[256,1000]{0,1:T(8,128)(2,1)S(1)} copy-done((bf16[256,1000]{0,1:T(8,128)(2,1)S(1)}, bf16[256,1000]{0,1:T(8,128)(2,1)}, u32[]{:S(2)}) %copy-start) | copy-done | bytes 512024
  1.7 0.0 copy-start.1
  1.7 0.8 %copy-done.1 = bf16[1000,16]{0,1:T(8,128)(2,1)S(1)} copy-done((bf16[1000,16]{0,1:T(8,128)(2,1)S(1)}, bf16[1000,16]{0,1:T(8,128)(2,1)}, u32[]{:S(2)}) %copy-start.1) | copy-done | bytes 32024
  2.5 0.0 copy-start.2
  2.5 0.8 %copy-done.2 = bf16[1000,16]{0,1:T(8,128)(2,1)S(1)} copy-done((bf16[1000,16]{0,1:T(8,128)(2,1)S(1)}, bf16[1000,16]{0,1:T(8,128)(2,1)}, u32[]{:S(2)}) %copy-start.2) | copy-done | bytes 32024
  3.3 65.7 %shard_map.64 = f32[16,1000]{1,0:T(8,128)S(1)} custom-call(bf16[1000,256]{1,0:T(8,128)(2,1)S(1)} %bitcast.6, bf16[16,1000]{1,0:T(8,128)(2,1)S(1)} %bitcast.8, bf16[16,1000]{1,0:T(8,128)(2,1)S(1)} %bitcast.9, f32[1,256]{1,0:T(1,128)S(1)} %bitcast.10, s32[1,8]{1,0:T(1,128)S(1)} %bitcast.11, s32[8,8]{1,0:T(8,128)S(1)} %copy-done.3), custom_call_target="tpu_custom_call" | custom-call | tf_op jit(solution)/shard_map/pallas_call | solution.py:310
  69.0 0.6 copy.8
Async XLA Ops:
  0.0 0.7 copy-start.3
  0.0 0.7 copy-start.4
  0.0 0.7 copy-start.5
  0.7 1.0 %copy-start = (bf16[256,1000]{0,1:T(8,128)(2,1)S(1)}, bf16[256,1000]{0,1:T(8,128)(2,1)}, u32[]{:S(2)}) copy-start(bf16[256,1000]{0,1:T(8,128)(2,1)} %param.6) | copy-start | bytes 1536004
  1.7 0.8 %copy-start.1 = (bf16[1000,16]{0,1:T(8,128)(2,1)S(1)}, bf16[1000,16]{0,1:T(8,128)(2,1)}, u32[]{:S(2)}) copy-start(bf16[1000,16]{0,1:T(8,128)(2,1)} %param.7) | copy-start | bytes 96004
  2.5 0.8 %copy-start.2 = (bf16[1000,16]{0,1:T(8,128)(2,1)S(1)}, bf16[1000,16]{0,1:T(8,128)(2,1)}, u32[]{:S(2)}) copy-start(bf16[1000,16]{0,1:T(8,128)(2,1)} %param.8) | copy-start | bytes 96004

commit v2 on v1

v2 whole, which is shorter than its diff:
```python
import functools
import math

import jax
import jax.numpy as jnp
from jax import lax
from jax.experimental import pallas as pl
from jax.experimental.pallas import tpu as pltpu
from jax.sharding import PartitionSpec as P

MESH = pl.DeviceIdType.MESH
NX, NYH, NYL, NZ, NC = 4, 4, 2, 8, 2
CAP = 32

SETS = (
    ((0, 0), (1, 0), (0, 1), (0, 7)),
    ((0, 2), (0, 6), (1, 1), (1, 7)),
    ((0, 3), (0, 5), (0, 4), (1, 2)),
    ((1, 6), (1, 3), (1, 5), (1, 4)),
)
WHERE = {slot: (s, i) for s, row in enumerate(SETS) for i, slot in enumerate(row)}


def kernel(
    v_hbm, occ_hbm, tri_hbm, w_hbm, sz_hbm, sig_hbm, out_ref,
    v_ref, w_ref, sz_ref, sig_ref, panels, vraw, sigp, smat, stran, prod,
    xin,
    turned, yrecv, dens_out, dens_in, kall,
    xsend, xrecv, zsend, zrecv,
    sems, p_sems, c_sems, x_sems, y_sems, k_sems, d_sems, l_sems,
    near, far, ready_x, ready_z, far_z,
):
    g, o = lax.axis_index("grid"), lax.axis_index("occ")
    yl, z, c = g // (NZ * NC), (g // NC) % NZ, g % NC
    x, yh = o // NYH, o % NYH
    nrow = occ_hbm.shape[0]
    npt = v_ref.shape[1]

    def grid_at(dy, dz, dc):
        return (((yl + dy) % NYL) * NZ + (z + dz) % NZ) * NC + (c + dc) % NC

    def occ_at(dx, dyh):
        return ((x + dx) % NX) * NYH + (yh + dyh) % NYH

    sent = []

    def send(src, dst, recv_sem, dy=0, dz=0, dc=0, dx=0, dyh=0):
        copy = pltpu.make_async_remote_copy(
            src_ref=src, dst_ref=dst, send_sem=sems.at[len(sent)], recv_sem=recv_sem,
            device_id=at(dy, dz, dc, dx, dyh), device_id_type=MESH,
        )
        copy.start()
        sent.append(copy)

    def arrive(dst, recv_sem):
        pltpu.make_async_remote_copy(
            src_ref=dst, dst_ref=dst, send_sem=sems.at[0], recv_sem=recv_sem,
            device_id=at(dc=1), device_id_type=MESH,
        ).wait_recv()

    own = (occ_hbm, tri_hbm)
    loads = [
        pltpu.make_async_copy(src, dst, l_sems.at[n])
        for n, (src, dst) in enumerate((
            (sig_hbm, sig_ref), (v_hbm, v_ref), (occ_hbm, panels.at[0, 0, 0]),
            (tri_hbm, panels.at[0, 1, 0]), (w_hbm, w_ref), (sz_hbm, sz_ref),
        ))
    ]
    for load in loads:
        load.start()

    def at(dy=0, dz=0, dc=0, dx=0, dyh=0):
        return {"grid": grid_at(dy, dz, dc), "occ": occ_at(dx, dyh)}

    def signal(sem, where):
        pl.semaphore_signal(sem, inc=1, device_id=where, device_id_type=MESH)

    beside = (at(dy=1, dyh=yl), at(dy=1, dyh=yl + NYH - 1))
    barrier = pltpu.get_barrier_semaphore()
    peers = (at(dc=1), at(dz=1), at(dz=7), at(dx=1), at(dx=3)) + beside
    for peer in peers:
        signal(barrier, peer)
    pl.semaphore_wait(barrier, len(peers))
    for peer in beside:
        signal(near, peer)
    for peer in (at(dx=1), at(dx=3)):
        signal(ready_x, peer)
    for peer in (at(dz=1), at(dz=7)):
        signal(ready_z, peer)

    def place(slot, t):
        s, i = WHERE[slot]
        return panels.at[s, t, i]

    def p_sem(slot, t):
        s, i = WHERE[slot]
        return p_sems.at[(s * 4 + i) * 2 + t]

    for t in range(2):
        send(own[t], place((0, 7), t), p_sem((0, 7), t), dz=1)
        send(own[t], place((0, 1), t), p_sem((0, 1), t), dz=7)
    for t in range(2):
        send(own[t], place((1, 0), t), p_sem((1, 0), t), dy=1)
    send(sig_hbm, sigp, c_sems.at[0], dc=1)
    send(v_hbm, vraw, c_sems.at[1], dc=1)
    pl.semaphore_wait(ready_z, 2)
    for step in (2, 6):
        signal(far_z, at(dz=step))

    def got(slot, t):
        arrive(place(slot, t), p_sem(slot, t))

    def relay(slot, t, moves):
        got(slot, t)
        for to, step in moves:
            send(place(slot, t), place(to, t), p_sem(to, t), **step)

    up, down, over = dict(dz=1), dict(dz=7), dict(dy=1)

    nblock, nbatch = sig_ref.shape[1], sig_ref.shape[0]
    width = v_ref.shape[0] // nblock

    def screen(values, significant):
        sig = significant.astype(jnp.float32).astype(jnp.bfloat16)
        eye = (
            lax.broadcasted_iota(jnp.int32, (nblock, nblock), 0)
            == lax.broadcasted_iota(jnp.int32, (nblock, nblock), 1)
        ).astype(jnp.bfloat16)
        flipped = lax.dot_general(
            eye, sig, (((1,), (1,)), ((), ())), preferred_element_type=jnp.float32
        ).astype(jnp.bfloat16)
        spread = (
            lax.broadcasted_iota(jnp.int32, (nbatch, npt), 1) // CAP
            == lax.broadcasted_iota(jnp.int32, (nbatch, npt), 0)
        ).astype(jnp.bfloat16)
        lanes = jnp.dot(flipped, spread, preferred_element_type=jnp.float32).astype(jnp.bfloat16)
        rows = (
            lax.broadcasted_iota(jnp.int32, (v_ref.shape[0], nblock), 0) // width
            == lax.broadcasted_iota(jnp.int32, (v_ref.shape[0], nblock), 1)
        ).astype(jnp.bfloat16)
        mask = jnp.dot(rows, lanes, preferred_element_type=jnp.float32)
        return values * mask.astype(jnp.bfloat16)

    for load in loads:
        load.wait()
    smat[c] = screen(v_ref[...], sig_ref[...])
    pl.semaphore_wait(far_z, 2)
    for t in range(2):
        send(own[t], place((0, 4), t), p_sem((0, 4), t), dz=4)

    for t in range(2):
        relay((0, 7), t, (((0, 6), up), ((1, 7), over)))
        relay((0, 1), t, (((0, 2), down), ((1, 1), over)))
    pl.semaphore_wait(near, 2)
    for k in (1, 3):
        signal(far, at(dyh=k))
    arrive(sigp, c_sems.at[0])
    arrive(vraw, c_sems.at[1])
    smat[1 - c] = screen(vraw[...], sigp[...])

    for k in range(NC):
        stran[k] = smat[k].T
    half = nrow * 4

    def multiply(s):
        lhs = panels[s].reshape(2 * half, v_ref.shape[0])
        for k in range(NC):
            res = jnp.dot(lhs, smat[k], preferred_element_type=jnp.float32)
            for h in range(2):
                prod[s, 2 * k + h] = res[:, h * 128 : (h + 1) * 128]

    def x_first(s):
        for d in (2, 1, 3):
            send(prod.at[s, (x + d) % NX], xin.at[s, d - 1], x_sems.at[s, d - 1], dx=d)

    def x_last(s):
        for d in range(1, NX):
            arrive(xin.at[s, d - 1], x_sems.at[s, d - 1])
        both = prod[s, x] + xin[s, 0] + xin[s, 1] + xin[s, 2]
        turned[s] = both.T.reshape(NYH, CAP, 2 * half)
        for k in (2, 1, 3):
            send(turned.at[s, (yh + k) % NYH], yrecv.at[s, k - 1], y_sems.at[s, k - 1], dyh=k)

    for t in range(2):
        got((1, 0), t)
    pl.semaphore_wait(ready_x, 2)
    multiply(0)
    x_first(0)
    for t in range(2):
        relay((0, 6), t, (((0, 5), up),))
        relay((0, 2), t, (((0, 3), down),))
    for t in range(2):
        relay((1, 7), t, (((1, 6), up),))
        relay((1, 1), t, (((1, 2), down),))
    multiply(1)
    x_first(1)
    pl.semaphore_wait(far, 2)
    for t in range(2):
        relay((0, 4), t, (((1, 4), over),))
    for t in range(2):
        relay((0, 5), t, (((1, 5), over),))
        relay((0, 3), t, (((1, 3), over),))
    for t in range(2):
        got((1, 2), t)
    multiply(2)
    x_first(2)
    x_last(0)
    for t in range(2):
        got((1, 6), t)
        got((1, 4), t)
        got((1, 5), t)
        got((1, 3), t)
    multiply(3)
    x_first(3)
    x_last(1)
    x_last(2)
    x_last(3)

    lane = lax.broadcasted_iota(jnp.int32, (CAP, 2 * half), 1)
    units, rolled = [], []
    part = jnp.zeros((CAP, 1), jnp.float32)
    for s in range(4):
        for k in range(1, NYH):
            arrive(yrecv.at[s, k - 1], y_sems.at[s, k - 1])
        unit = turned[s, yh] + yrecv[s, 0] + yrecv[s, 1] + yrecv[s, 2]
        other = pltpu.roll(unit, half, 1)
        units.append(unit)
        rolled.append(other)
        part += jnp.sum(jnp.where(lane < half, unit * other, 0.0), axis=1, keepdims=True)

    batch = o % nbatch
    row_of = lax.broadcasted_iota(jnp.int32, (CAP, npt), 0)
    lane_of = lax.broadcasted_iota(jnp.int32, (CAP, npt), 1)
    weight = jnp.sum(
        jnp.where(lane_of == row_of + batch * CAP, w_ref[...], 0.0), axis=1, keepdims=True
    )
    count = jnp.sum(
        jnp.where(
            lax.broadcasted_iota(jnp.int32, (1, nbatch), 1) == batch,
            sz_ref[...].astype(jnp.float32), 0.0,
        ),
        axis=1, keepdims=True,
    )
    live = lax.broadcasted_iota(jnp.int32, (CAP, 1), 0).astype(jnp.float32) < count
    weight = jnp.where(live, weight, 0.0)
    dens_out[...] = jnp.where(lane < half, part, weight)
    send(dens_out, dens_in, d_sems.at[0], dc=1)
    arrive(dens_in, d_sems.at[0])
    total = 2 * nrow * NYL * NZ
    density = (part + dens_in[:, 0:1]) * (1.0 / math.sqrt(total))
    weight = jnp.where(o // nbatch == c, weight, dens_in[:, half : half + 1])
    for p in range(2):
        a, b = 2 * p, 2 * p + 1
        value = jnp.where(
            lane < half, density * units[a] + rolled[a], density * rolled[b] + units[b]
        )
        kall[p, o] = (weight * value).astype(jnp.bfloat16)

    def k_from(p, dx, dyh):
        return kall.at[p, occ_at(dx, dyh)]

    for p in (1, 0):
        for k in (2, 1, 3):
            send(k_from(p, 0, 0), k_from(p, 0, 0), k_sems.at[p, 0, NYH - k], dyh=k)
    for p in (1, 0):
        for k in (0, 1, 3, 2):
            if k:
                arrive(k_from(p, 0, k), k_sems.at[p, 0, k])
            for d in (2, 1, 3):
                send(k_from(p, 0, k), k_from(p, 0, k), k_sems.at[p, NX - d, k], dx=d)
    held = {}
    for p in (1, 0):
        for k in (0, 1, 3, 2):
            for d in (1, 3, 2):
                arrive(k_from(p, d, k), k_sems.at[p, d, k])
        kt = kall[p].reshape(2 * npt, 2 * half).T
        res = sum(
            jnp.dot(
                kt[:, k * npt : (k + 1) * npt], stran[k], preferred_element_type=jnp.float32
            )
            for k in range(NC)
        )
        slots = SETS[2 * p] + SETS[2 * p + 1]
        for dz in (4, 3, 5, 2, 6, 1, 7, 0):
            for dy in (1, 0):
                if (dy, dz) in slots:
                    i = slots.index((dy, dz))
                    block = res[i * nrow : (i + 1) * nrow]
                    if dy:
                        xsend[dz] = block.astype(jnp.bfloat16)
                        send(xsend.at[dz], xrecv.at[dz], d_sems.at[1 + dz], dy=1)
                    else:
                        held[dz] = block
    mine = None
    for dz in (4, 3, 5, 2, 6, 1, 7, 0):
        arrive(xrecv.at[dz], d_sems.at[1 + dz])
        value = held[dz] + xrecv[dz].astype(jnp.float32)
        if dz:
            zsend[dz - 1] = value.astype(jnp.bfloat16)
            send(zsend.at[dz - 1], zrecv.at[dz - 1], d_sems.at[8 + dz], dz=dz)
        else:
            mine = value
    for dz in (1, 7, 2, 6, 3, 5, 4):
        arrive(zrecv.at[dz - 1], d_sems.at[8 + dz])
        mine = mine + zrecv[dz - 1].astype(jnp.float32)
    points = npt * NYL * NZ * NC
    out_ref[...] = mine * (1.0 / math.sqrt(points))
    for copy in sent:
        copy.wait_send()


def per_device(orbital_values, occupied, trial, point_weights, batch_sizes, significant):
    v, occ, tri = orbital_values.T, occupied.T, trial.T
    m, npt = v.shape
    nrow = occ.shape[0]
    half = 4 * nrow
    f32, bf16 = jnp.float32, jnp.bfloat16
    dma = pltpu.SemaphoreType.DMA
    out = pl.pallas_call(
        kernel,
        out_shape=jax.ShapeDtypeStruct((nrow, m), f32),
        in_specs=[pl.BlockSpec(memory_space=pl.ANY)] * 6,
        out_specs=pl.BlockSpec(memory_space=pltpu.VMEM),
        scratch_shapes=[
            pltpu.VMEM((m, npt), bf16),
            pltpu.VMEM((1, npt), f32),
            pltpu.VMEM((1, batch_sizes.shape[0]), jnp.int32),
            pltpu.VMEM(significant.shape, jnp.int32),
            pltpu.VMEM((4, 2, 4, nrow, m), bf16),
            pltpu.VMEM((m, npt), bf16),
            pltpu.VMEM(significant.shape, jnp.int32),
            pltpu.VMEM((NC, m, npt), bf16),
            pltpu.VMEM((NC, npt, m), bf16),
            pltpu.VMEM((4, NX, 2 * half, 128), f32),
        ]
        + [
            pltpu.VMEM((4, NX - 1, 2 * half, 128), f32),
            pltpu.VMEM((4, NYH, CAP, 2 * half), f32),
            pltpu.VMEM((4, NYH - 1, CAP, 2 * half), f32),
            pltpu.VMEM((CAP, 2 * half), f32),
            pltpu.VMEM((CAP, 2 * half), f32),
            pltpu.VMEM((2, NX * NYH, CAP, 2 * half), bf16),
            pltpu.VMEM((NZ, nrow, m), bf16),
            pltpu.VMEM((NZ, nrow, m), bf16),
            pltpu.VMEM((NZ - 1, nrow, m), bf16),
            pltpu.VMEM((NZ - 1, nrow, m), bf16),
            dma((160,)),
            dma((32,)),
            dma((2,)),
            dma((4, NX - 1)),
            dma((4, NYH - 1)),
            dma((2, NX, NYH)),
            dma((1 + 8 + 8,)),
            dma((6,)),
        ]
        + [pltpu.SemaphoreType.REGULAR] * 5,
        compiler_params=pltpu.CompilerParams(
            collective_id=0, has_side_effects=True, vmem_limit_bytes=24 << 20
        ),
    )(*(
        pltpu.with_memory_space_constraint(a, pltpu.HBM)
        for a in (v, occ, tri, point_weights.reshape(1, -1), batch_sizes.reshape(1, -1), significant)
    ))
    return out.T


def solution(mesh):
    placed = (
        P("grid", "occ"),
        P("occ", "grid"),
        P("occ", "grid"),
        P("grid"),
        P("grid"),
        P("grid", "occ"),
    )
    return jax.shard_map(
        per_device, mesh=mesh, in_specs=placed, out_specs=P("occ", "grid"), check_vma=False
    )
```

time: 70.9 us -> 62.8 us (0.89); the launches traced: 69.6 us -> 62.6 us
  Pallas kernels: 65.7 us -> 62 us
  local copies, waits for them, and re-layouts: 3.88 us -> 0.63 us
    pallas_call x1, Pallas kernels: 65.7 us -> 62 us  [per_device(): pl.pallas_call(kernel, out_shape=jax.ShapeDtypeStruct((nrow, m), f32), in...]
    unnamed x13 -> x1, local copies, waits for them, and re-layouts: 3.88 us -> 0.63 us
where the time goes in v2:
time: 62.8 us; the launch traced here: 62.6 us
  Pallas kernels  62 us (99%)
  local copies, waits for them, and re-layouts  0.63 us (1%)
    pallas_call x1, Pallas kernels, per_device(): pl.pallas_call(kernel, out_shape=jax.ShapeDtypeStruct((nrow, m), f32), in...  62 us

profile of v2, /device:TPU:1, one launch (start us, length us, event | category | flops | bytes accessed | tf_op | source)
XLA Modules:
  0.0 62.6 jit_solution(1339402667005947049)
XLA Ops:
  0.0 62.0 %shard_map.64 = f32[16,1000]{1,0:T(8,128)S(1)} custom-call(bf16[1000,256]{1,0:T(8,128)(2,1)} %bitcast.7, bf16[16,1000]{1,0:T(8,128)(2,1)} %bitcast.8, bf16[16,1000]{1,0:T(8,128)(2,1)} %bitcast.9, f32[1,256]{1,0:T(1,128)} %bitcast.10, s32[1,8]{1,0:T(1,128)} %bitcast.11, s32[8,8]{1,0:T(8,128)} %sig_hbm.1), custom_call_target="tpu_custom_call" | custom-call | tf_op jit(solution)/shard_map/pallas_call | solution.py:319
  62.0 0.6 %copy.8 = f32[1000,16]{0,1:T(8,128)} copy(f32[1000,16]{0,1:T(8,128)S(1)} %bitcast.6) | data formatting | bytes 128000

commit v3 on v2

--- a/solution.py
+++ b/solution.py
@@ -15,15 +15,15 @@
 SETS = (
     ((0, 0), (1, 0), (0, 1), (0, 7)),
     ((0, 2), (0, 6), (1, 1), (1, 7)),
-    ((0, 3), (0, 5), (0, 4), (1, 2)),
-    ((1, 6), (1, 3), (1, 5), (1, 4)),
+    ((0, 4), (0, 3), (1, 2), (1, 6)),
+    ((0, 5), (1, 4), (1, 3), (1, 5)),
 )
 WHERE = {slot: (s, i) for s, row in enumerate(SETS) for i, slot in enumerate(row)}
 
 
 def kernel(
     v_hbm, occ_hbm, tri_hbm, w_hbm, sz_hbm, sig_hbm, out_ref,
-    v_ref, w_ref, sz_ref, sig_ref, panels, vraw, sigp, smat, stran, prod,
+    v_ref, w_ref, sz_ref, sig_ref, mine_ref, panels, vraw, sigp, smat, stran, prod,
     xin,
     turned, yrecv, dens_out, dens_in, kall,
     xsend, xrecv, zsend, zrecv,
@@ -58,16 +58,17 @@
             device_id=at(dc=1), device_id_type=MESH,
         ).wait_recv()
 
-    own = (occ_hbm, tri_hbm)
+    m, wide = v_hbm.shape[0], panels.shape[-1]
     loads = [
         pltpu.make_async_copy(src, dst, l_sems.at[n])
         for n, (src, dst) in enumerate((
-            (sig_hbm, sig_ref), (v_hbm, v_ref), (occ_hbm, panels.at[0, 0, 0]),
-            (tri_hbm, panels.at[0, 1, 0]), (w_hbm, w_ref), (sz_hbm, sz_ref),
+            (occ_hbm, mine_ref.at[0]), (tri_hbm, mine_ref.at[1]), (sig_hbm, sig_ref),
+            (v_hbm, v_ref), (w_hbm, w_ref), (sz_hbm, sz_ref),
         ))
     ]
     for load in loads:
         load.start()
+    smat[:, m:] = jnp.zeros((NC, wide - m, npt), smat.dtype)
 
     def at(dy=0, dz=0, dc=0, dx=0, dyh=0):
         return {"grid": grid_at(dy, dz, dc), "occ": occ_at(dx, dyh)}
@@ -80,6 +81,10 @@
     peers = (at(dc=1), at(dz=1), at(dz=7), at(dx=1), at(dx=3)) + beside
     for peer in peers:
         signal(barrier, peer)
+    for load in loads:
+        load.wait()
+    panels[0, :, 0, :, :m] = mine_ref[...]
+    panels[0, :, 0, :, m:] = jnp.zeros((2, nrow, wide - m), panels.dtype)
     pl.semaphore_wait(barrier, len(peers))
     for peer in beside:
         signal(near, peer)
@@ -88,32 +93,33 @@
     for peer in (at(dz=1), at(dz=7)):
         signal(ready_z, peer)
 
-    def place(slot, t):
+    def place(slot, q):
         s, i = WHERE[slot]
-        return panels.at[s, t, i]
-
-    def p_sem(slot, t):
+        return panels.at[s, q // 2, i, :, pl.ds((q % 2) * (wide // 2), wide // 2)]
+
+    def p_sem(slot, q):
         s, i = WHERE[slot]
-        return p_sems.at[(s * 4 + i) * 2 + t]
-
-    for t in range(2):
-        send(own[t], place((0, 7), t), p_sem((0, 7), t), dz=1)
-        send(own[t], place((0, 1), t), p_sem((0, 1), t), dz=7)
-    for t in range(2):
-        send(own[t], place((1, 0), t), p_sem((1, 0), t), dy=1)
+        return p_sems.at[(s * 4 + i) * 4 + q]
+
+    for q in range(4):
+        send(place((0, 0), q), place((0, 7), q), p_sem((0, 7), q), dz=1)
+        send(place((0, 0), q), place((0, 1), q), p_sem((0, 1), q), dz=7)
+        send(place((0, 0), q), place((1, 0), q), p_sem((1, 0), q), dy=1)
     send(sig_hbm, sigp, c_sems.at[0], dc=1)
     send(v_hbm, vraw, c_sems.at[1], dc=1)
     pl.semaphore_wait(ready_z, 2)
     for step in (2, 6):
         signal(far_z, at(dz=step))
 
-    def got(slot, t):
-        arrive(place(slot, t), p_sem(slot, t))
-
-    def relay(slot, t, moves):
-        got(slot, t)
+    def got(*slots):
+        for slot in slots:
+            for q in range(4):
+                arrive(place(slot, q), p_sem(slot, q))
+
+    def relay(slot, q, *moves):
+        arrive(place(slot, q), p_sem(slot, q))
         for to, step in moves:
-            send(place(slot, t), place(to, t), p_sem(to, t), **step)
+            send(place(slot, q), place(to, q), p_sem(to, q), **step)
 
     up, down, over = dict(dz=1), dict(dz=7), dict(dy=1)
 
@@ -141,29 +147,23 @@
         mask = jnp.dot(rows, lanes, preferred_element_type=jnp.float32)
         return values * mask.astype(jnp.bfloat16)
 
-    for load in loads:
-        load.wait()
-    smat[c] = screen(v_ref[...], sig_ref[...])
-    pl.semaphore_wait(far_z, 2)
-    for t in range(2):
-        send(own[t], place((0, 4), t), p_sem((0, 4), t), dz=4)
-
-    for t in range(2):
-        relay((0, 7), t, (((0, 6), up), ((1, 7), over)))
-        relay((0, 1), t, (((0, 2), down), ((1, 1), over)))
+    smat[c, :m] = screen(v_ref[...], sig_ref[...])
     pl.semaphore_wait(near, 2)
     for k in (1, 3):
         signal(far, at(dyh=k))
     arrive(sigp, c_sems.at[0])
     arrive(vraw, c_sems.at[1])
-    smat[1 - c] = screen(vraw[...], sigp[...])
-
+    smat[1 - c, :m] = screen(vraw[...], sigp[...])
+    pl.semaphore_wait(far_z, 2)
+    for q in range(4):
+        relay((0, 7), q, ((0, 6), up), ((1, 7), over), *([((0, 4), dict(dz=3))] if q < 2 else []))
+        relay((0, 1), q, ((0, 2), down), ((1, 1), over), *([((0, 4), dict(dz=5))] if q > 1 else []))
     for k in range(NC):
         stran[k] = smat[k].T
     half = nrow * 4
 
     def multiply(s):
-        lhs = panels[s].reshape(2 * half, v_ref.shape[0])
+        lhs = panels[s].reshape(2 * half, wide)
         for k in range(NC):
             res = jnp.dot(lhs, smat[k], preferred_element_type=jnp.float32)
             for h in range(2):
@@ -181,35 +181,25 @@
         for k in (2, 1, 3):
             send(turned.at[s, (yh + k) % NYH], yrecv.at[s, k - 1], y_sems.at[s, k - 1], dyh=k)
 
-    for t in range(2):
-        got((1, 0), t)
+    got((1, 0))
     pl.semaphore_wait(ready_x, 2)
     multiply(0)
     x_first(0)
-    for t in range(2):
-        relay((0, 6), t, (((0, 5), up),))
-        relay((0, 2), t, (((0, 3), down),))
-    for t in range(2):
-        relay((1, 7), t, (((1, 6), up),))
-        relay((1, 1), t, (((1, 2), down),))
+    for q in range(4):
+        relay((0, 6), q, ((0, 5), up), ((1, 6), over))
+        relay((0, 2), q, ((0, 3), down), ((1, 2), over))
+        relay((1, 7), q, ((1, 5), dict(dz=2)))
+        relay((1, 1), q, ((1, 3), dict(dz=6)))
     multiply(1)
     x_first(1)
     pl.semaphore_wait(far, 2)
-    for t in range(2):
-        relay((0, 4), t, (((1, 4), over),))
-    for t in range(2):
-        relay((0, 5), t, (((1, 5), over),))
-        relay((0, 3), t, (((1, 3), over),))
-    for t in range(2):
-        got((1, 2), t)
+    for q in (2, 0, 1, 3):
+        relay((0, 4), q, ((1, 4), over))
+    got((1, 2), (1, 6), (0, 3))
     multiply(2)
     x_first(2)
     x_last(0)
-    for t in range(2):
-        got((1, 6), t)
-        got((1, 4), t)
-        got((1, 5), t)
-        got((1, 3), t)
+    got((0, 5), (1, 4), (1, 5), (1, 3))
     multiply(3)
     x_first(3)
     x_last(1)
@@ -304,7 +294,7 @@
         arrive(zrecv.at[dz - 1], d_sems.at[8 + dz])
         mine = mine + zrecv[dz - 1].astype(jnp.float32)
     points = npt * NYL * NZ * NC
-    out_ref[...] = mine * (1.0 / math.sqrt(points))
+    out_ref[...] = mine[:, :m] * (1.0 / math.sqrt(points))
     for copy in sent:
         copy.wait_send()
 
@@ -314,6 +304,7 @@
     m, npt = v.shape
     nrow = occ.shape[0]
     half = 4 * nrow
+    wide = (m + 127) // 128 * 128
     f32, bf16 = jnp.float32, jnp.bfloat16
     dma = pltpu.SemaphoreType.DMA
     out = pl.pallas_call(
@@ -326,11 +317,12 @@
             pltpu.VMEM((1, npt), f32),
             pltpu.VMEM((1, batch_sizes.shape[0]), jnp.int32),
             pltpu.VMEM(significant.shape, jnp.int32),
-            pltpu.VMEM((4, 2, 4, nrow, m), bf16),
+            pltpu.VMEM((2, nrow, m), bf16),
+            pltpu.VMEM((4, 2, 4, nrow, wide), bf16),
             pltpu.VMEM((m, npt), bf16),
             pltpu.VMEM(significant.shape, jnp.int32),
-            pltpu.VMEM((NC, m, npt), bf16),
-            pltpu.VMEM((NC, npt, m), bf16),
+            pltpu.VMEM((NC, wide, npt), bf16),
+            pltpu.VMEM((NC, npt, wide), bf16),
             pltpu.VMEM((4, NX, 2 * half, 128), f32),
         ]
         + [
@@ -340,12 +332,12 @@
             pltpu.VMEM((CAP, 2 * half), f32),
             pltpu.VMEM((CAP, 2 * half), f32),
             pltpu.VMEM((2, NX * NYH, CAP, 2 * half), bf16),
-            pltpu.VMEM((NZ, nrow, m), bf16),
-            pltpu.VMEM((NZ, nrow, m), bf16),
-            pltpu.VMEM((NZ - 1, nrow, m), bf16),
-            pltpu.VMEM((NZ - 1, nrow, m), bf16),
-            dma((160,)),
-            dma((32,)),
+            pltpu.VMEM((NZ, nrow, wide), bf16),
+            pltpu.VMEM((NZ, nrow, wide), bf16),
+            pltpu.VMEM((NZ - 1, nrow, wide), bf16),
+            pltpu.VMEM((NZ - 1, nrow, wide), bf16),
+            dma((192,)),
+            dma((64,)),
             dma((2,)),
             dma((4, NX - 1)),
             dma((4, NYH - 1)),

time: 62.8 us -> 60.4 us (0.962)
  Pallas kernels: 62 us -> 59.6 us
    pallas_call x1, Pallas kernels: 62 us -> 59.6 us  [per_device(): pl.pallas_call(kernel, out_shape=jax.ShapeDtypeStruct((nrow, m), f32), in...]
where the time goes in v3:
time: 60.4 us; the launch traced here: 60.2 us
  Pallas kernels  59.6 us (99%)
  local copies, waits for them, and re-layouts  0.63 us (1%)
    pallas_call x1, Pallas kernels, per_device(): pl.pallas_call(kernel, out_shape=jax.ShapeDtypeStruct((nrow, m), f32), in...  59.6 us

profile of v3, /device:TPU:1, one launch (start us, length us, event | category | flops | bytes accessed | tf_op | source)
XLA Modules:
  0.0 60.2 jit_solution(15181154266115011662)
XLA Ops:
  0.0 59.6 %shard_map.64 = f32[16,1000]{1,0:T(8,128)S(1)} custom-call(bf16[1000,256]{1,0:T(8,128)(2,1)} %bitcast.7, bf16[16,1000]{1,0:T(8,128)(2,1)} %bitcast.8, bf16[16,1000]{1,0:T(8,128)(2,1)} %bitcast.9, f32[1,256]{1,0:T(1,128)} %bitcast.10, s32[1,8]{1,0:T(1,128)} %bitcast.11, s32[8,8]{1,0:T(8,128)} %sig_hbm.1), custom_call_target="tpu_custom_call" | custom-call | tf_op jit(solution)/shard_map/pallas_call | solution.py:310
  59.6 0.6 %copy.8 = f32[1000,16]{0,1:T(8,128)} copy(f32[1000,16]{0,1:T(8,128)S(1)} %bitcast.6) | data formatting | bytes 128000

commit v4 on v3

--- a/solution.py
+++ b/solution.py
@@ -23,12 +23,12 @@
 
 def kernel(
     v_hbm, occ_hbm, tri_hbm, w_hbm, sz_hbm, sig_hbm, out_ref,
-    v_ref, w_ref, sz_ref, sig_ref, mine_ref, panels, vraw, sigp, smat, stran, prod,
-    xin,
+    v_ref, w_ref, sz_ref, sig_ref, mine_ref, panels, vraw, sigp, stran, prod,
+    xin, oin,
     turned, yrecv, dens_out, dens_in, kall,
     xsend, xrecv, zsend, zrecv,
-    sems, p_sems, c_sems, x_sems, y_sems, k_sems, d_sems, l_sems,
-    near, far, ready_x, ready_z, far_z,
+    sems, p_sems, c_sems, x_sems, e_sems, o_sems, y_sems, k_sems, d_sems, l_sems,
+    near, far, ready_x, ready_z, far_z, cross,
 ):
     g, o = lax.axis_index("grid"), lax.axis_index("occ")
     yl, z, c = g // (NZ * NC), (g // NC) % NZ, g % NC
@@ -68,7 +68,7 @@
     ]
     for load in loads:
         load.start()
-    smat[:, m:] = jnp.zeros((NC, wide - m, npt), smat.dtype)
+    stran[:, :, m:] = jnp.zeros((NC, npt, wide - m), stran.dtype)
 
     def at(dy=0, dz=0, dc=0, dx=0, dyh=0):
         return {"grid": grid_at(dy, dz, dc), "occ": occ_at(dx, dyh)}
@@ -147,27 +147,29 @@
         mask = jnp.dot(rows, lanes, preferred_element_type=jnp.float32)
         return values * mask.astype(jnp.bfloat16)
 
-    smat[c, :m] = screen(v_ref[...], sig_ref[...])
+    stran[c, :, :m] = screen(v_ref[...], sig_ref[...]).T
     pl.semaphore_wait(near, 2)
     for k in (1, 3):
         signal(far, at(dyh=k))
     arrive(sigp, c_sems.at[0])
     arrive(vraw, c_sems.at[1])
-    smat[1 - c, :m] = screen(vraw[...], sigp[...])
+    stran[1 - c, :, :m] = screen(vraw[...], sigp[...]).T
     pl.semaphore_wait(far_z, 2)
     for q in range(4):
         relay((0, 7), q, ((0, 6), up), ((1, 7), over), *([((0, 4), dict(dz=3))] if q < 2 else []))
         relay((0, 1), q, ((0, 2), down), ((1, 1), over), *([((0, 4), dict(dz=5))] if q > 1 else []))
-    for k in range(NC):
-        stran[k] = smat[k].T
     half = nrow * 4
 
     def multiply(s):
-        lhs = panels[s].reshape(2 * half, wide)
+        panel = panels[s].reshape(2 * half, wide)
         for k in range(NC):
-            res = jnp.dot(lhs, smat[k], preferred_element_type=jnp.float32)
-            for h in range(2):
-                prod[s, 2 * k + h] = res[:, h * 128 : (h + 1) * 128]
+            res = lax.dot_general(
+                stran[k], panel, (((1,), (1,)), ((), ())), preferred_element_type=jnp.float32
+            )
+            prod[s, 2 * k : 2 * k + 2] = res.reshape(2, NYH, CAP, 2 * half)
+
+    def block(s, d, k):
+        return prod.at[s, (x + d) % NX, (yh + k) % NYH]
 
     def x_first(s):
         for d in (2, 1, 3):
@@ -176,15 +178,32 @@
     def x_last(s):
         for d in range(1, NX):
             arrive(xin.at[s, d - 1], x_sems.at[s, d - 1])
-        both = prod[s, x] + xin[s, 0] + xin[s, 1] + xin[s, 2]
-        turned[s] = both.T.reshape(NYH, CAP, 2 * half)
+        turned[s] = prod[s, x] + xin[s, 0] + xin[s, 1] + xin[s, 2]
         for k in (2, 1, 3):
             send(turned.at[s, (yh + k) % NYH], yrecv.at[s, k - 1], y_sems.at[s, k - 1], dyh=k)
+
+    def x_first_short(s):
+        for d in (2, 1, 3, 0):
+            send(block(s, d, 2), oin.at[d], o_sems.at[d], dx=d, dyh=2)
+        for n, k in enumerate((1, 3, 0)):
+            for d in (2, 1, 3):
+                send(block(s, d, k), xin.at[s, d - 1, n], e_sems.at[d - 1, n], dx=d)
+
+    def x_last_short(s):
+        for n, k in enumerate((1, 3, 0)):
+            for d in range(1, NX):
+                arrive(xin.at[s, d - 1, n], e_sems.at[d - 1, n])
+            turned[s, n] = prod[s, x, (yh + k) % NYH] + xin[s, 0, n] + xin[s, 1, n] + xin[s, 2, n]
+            if k:
+                send(turned.at[s, n], yrecv.at[s, k - 1], y_sems.at[s, k - 1], dyh=k)
 
     got((1, 0))
     pl.semaphore_wait(ready_x, 2)
     multiply(0)
     x_first(0)
+    pl.semaphore_wait(far, 2)
+    for d in (2, 1, 3):
+        signal(cross, at(dx=d))
     for q in range(4):
         relay((0, 6), q, ((0, 5), up), ((1, 6), over))
         relay((0, 2), q, ((0, 3), down), ((1, 2), over))
@@ -192,7 +211,7 @@
         relay((1, 1), q, ((1, 3), dict(dz=6)))
     multiply(1)
     x_first(1)
-    pl.semaphore_wait(far, 2)
+    pl.semaphore_wait(cross, 3)
     for q in (2, 0, 1, 3):
         relay((0, 4), q, ((1, 4), over))
     got((1, 2), (1, 6), (0, 3))
@@ -201,18 +220,24 @@
     x_last(0)
     got((0, 5), (1, 4), (1, 5), (1, 3))
     multiply(3)
-    x_first(3)
+    x_first_short(3)
     x_last(1)
     x_last(2)
-    x_last(3)
+    x_last_short(3)
 
     lane = lax.broadcasted_iota(jnp.int32, (CAP, 2 * half), 1)
     units, rolled = [], []
     part = jnp.zeros((CAP, 1), jnp.float32)
     for s in range(4):
-        for k in range(1, NYH):
-            arrive(yrecv.at[s, k - 1], y_sems.at[s, k - 1])
-        unit = turned[s, yh] + yrecv[s, 0] + yrecv[s, 1] + yrecv[s, 2]
+        unit = turned[s, yh] if s < 3 else turned[s, 2]
+        for k in (1, 2, 3):
+            if s < 3 or k != 2:
+                arrive(yrecv.at[s, k - 1], y_sems.at[s, k - 1])
+                unit = unit + yrecv[s, k - 1]
+            else:
+                for d in range(NX):
+                    arrive(oin.at[d], o_sems.at[d])
+                    unit = unit + oin[d]
         other = pltpu.roll(unit, half, 1)
         units.append(unit)
         rolled.append(other)
@@ -290,13 +315,13 @@
             send(zsend.at[dz - 1], zrecv.at[dz - 1], d_sems.at[8 + dz], dz=dz)
         else:
             mine = value
+    for copy in sent:
+        copy.wait_send()
     for dz in (1, 7, 2, 6, 3, 5, 4):
         arrive(zrecv.at[dz - 1], d_sems.at[8 + dz])
         mine = mine + zrecv[dz - 1].astype(jnp.float32)
     points = npt * NYL * NZ * NC
     out_ref[...] = mine[:, :m] * (1.0 / math.sqrt(points))
-    for copy in sent:
-        copy.wait_send()
 
 
 def per_device(orbital_values, occupied, trial, point_weights, batch_sizes, significant):
@@ -321,12 +346,12 @@
             pltpu.VMEM((4, 2, 4, nrow, wide), bf16),
             pltpu.VMEM((m, npt), bf16),
             pltpu.VMEM(significant.shape, jnp.int32),
-            pltpu.VMEM((NC, wide, npt), bf16),
             pltpu.VMEM((NC, npt, wide), bf16),
-            pltpu.VMEM((4, NX, 2 * half, 128), f32),
+            pltpu.VMEM((4, NX, NYH, CAP, 2 * half), f32),
         ]
         + [
-            pltpu.VMEM((4, NX - 1, 2 * half, 128), f32),
+            pltpu.VMEM((4, NX - 1, NYH, CAP, 2 * half), f32),
+            pltpu.VMEM((NX, CAP, 2 * half), f32),
             pltpu.VMEM((4, NYH, CAP, 2 * half), f32),
             pltpu.VMEM((4, NYH - 1, CAP, 2 * half), f32),
             pltpu.VMEM((CAP, 2 * half), f32),
@@ -339,13 +364,15 @@
             dma((192,)),
             dma((64,)),
             dma((2,)),
-            dma((4, NX - 1)),
+            dma((3, NX - 1)),
+            dma((NX - 1, 3)),
+            dma((NX,)),
             dma((4, NYH - 1)),
             dma((2, NX, NYH)),
             dma((1 + 8 + 8,)),
             dma((6,)),
         ]
-        + [pltpu.SemaphoreType.REGULAR] * 5,
+        + [pltpu.SemaphoreType.REGULAR] * 6,
         compiler_params=pltpu.CompilerParams(
             collective_id=0, has_side_effects=True, vmem_limit_bytes=24 << 20
         ),

time: 60.4 us -> 59.9 us (level)
  no operation moved by 1% of the time
where the time goes in v4:
time: 59.9 us; the launch traced here: 59.8 us
  Pallas kernels  59.2 us (99%)
  local copies, waits for them, and re-layouts  0.63 us (1%)
    pallas_call x1, Pallas kernels, per_device(): pl.pallas_call(kernel, out_shape=jax.ShapeDtypeStruct((nrow, m), f32), in...  59.2 us

profile of v4, /device:TPU:1, one launch (start us, length us, event | category | flops | bytes accessed | tf_op | source)
XLA Modules:
  0.0 59.8 jit_solution(16164255008540616200)
XLA Ops:
  0.0 59.2 %shard_map.64 = f32[16,1000]{1,0:T(8,128)S(1)} custom-call(bf16[1000,256]{1,0:T(8,128)(2,1)} %bitcast.7, bf16[16,1000]{1,0:T(8,128)(2,1)} %bitcast.8, bf16[16,1000]{1,0:T(8,128)(2,1)} %bitcast.9, f32[1,256]{1,0:T(1,128)} %bitcast.10, s32[1,8]{1,0:T(1,128)} %bitcast.11, s32[8,8]{1,0:T(8,128)} %sig_hbm.1), custom_call_target="tpu_custom_call" | custom-call | tf_op jit(solution)/shard_map/pallas_call | solution.py:335
  59.2 0.6 %copy.8 = f32[1000,16]{0,1:T(8,128)} copy(f32[1000,16]{0,1:T(8,128)S(1)} %bitcast.6) | data formatting | bytes 128000

commit v5 on v4

--- a/solution.py
+++ b/solution.py
@@ -68,7 +68,6 @@
     ]
     for load in loads:
         load.start()
-    stran[:, :, m:] = jnp.zeros((NC, npt, wide - m), stran.dtype)
 
     def at(dy=0, dz=0, dc=0, dx=0, dyh=0):
         return {"grid": grid_at(dy, dz, dc), "occ": occ_at(dx, dyh)}
@@ -81,10 +80,6 @@
     peers = (at(dc=1), at(dz=1), at(dz=7), at(dx=1), at(dx=3)) + beside
     for peer in peers:
         signal(barrier, peer)
-    for load in loads:
-        load.wait()
-    panels[0, :, 0, :, :m] = mine_ref[...]
-    panels[0, :, 0, :, m:] = jnp.zeros((2, nrow, wide - m), panels.dtype)
     pl.semaphore_wait(barrier, len(peers))
     for peer in beside:
         signal(near, peer)
@@ -101,10 +96,19 @@
         s, i = WHERE[slot]
         return p_sems.at[(s * 4 + i) * 4 + q]
 
-    for q in range(4):
-        send(place((0, 0), q), place((0, 7), q), p_sem((0, 7), q), dz=1)
-        send(place((0, 0), q), place((0, 1), q), p_sem((0, 1), q), dz=7)
-        send(place((0, 0), q), place((1, 0), q), p_sem((1, 0), q), dy=1)
+    def leave(own, q):
+        send(own, place((0, 7), q), p_sem((0, 7), q), dz=1)
+        send(own, place((0, 1), q), p_sem((0, 1), q), dz=7)
+        send(own, place((1, 0), q), p_sem((1, 0), q), dy=1)
+
+    leave(occ_hbm.at[:, pl.ds(0, wide // 2)], 0)
+    leave(tri_hbm.at[:, pl.ds(0, wide // 2)], 2)
+    for load in loads[:2]:
+        load.wait()
+    panels[0, :, 0, :, :m] = mine_ref[...]
+    panels[0, :, 0, :, m:] = jnp.zeros((2, nrow, wide - m), panels.dtype)
+    for q in (1, 3):
+        leave(place((0, 0), q), q)
     send(sig_hbm, sigp, c_sems.at[0], dc=1)
     send(v_hbm, vraw, c_sems.at[1], dc=1)
     pl.semaphore_wait(ready_z, 2)
@@ -147,6 +151,9 @@
         mask = jnp.dot(rows, lanes, preferred_element_type=jnp.float32)
         return values * mask.astype(jnp.bfloat16)
 
+    for load in loads[2:]:
+        load.wait()
+    stran[:, :, m:] = jnp.zeros((NC, npt, wide - m), stran.dtype)
     stran[c, :, :m] = screen(v_ref[...], sig_ref[...]).T
     pl.semaphore_wait(near, 2)
     for k in (1, 3):
@@ -155,7 +162,7 @@
     arrive(vraw, c_sems.at[1])
     stran[1 - c, :, :m] = screen(vraw[...], sigp[...]).T
     pl.semaphore_wait(far_z, 2)
-    for q in range(4):
+    for q in (0, 2, 1, 3):
         relay((0, 7), q, ((0, 6), up), ((1, 7), over), *([((0, 4), dict(dz=3))] if q < 2 else []))
         relay((0, 1), q, ((0, 2), down), ((1, 1), over), *([((0, 4), dict(dz=5))] if q > 1 else []))
     half = nrow * 4
@@ -183,11 +190,13 @@
             send(turned.at[s, (yh + k) % NYH], yrecv.at[s, k - 1], y_sems.at[s, k - 1], dyh=k)
 
     def x_first_short(s):
-        for d in (2, 1, 3, 0):
-            send(block(s, d, 2), oin.at[d], o_sems.at[d], dx=d, dyh=2)
-        for n, k in enumerate((1, 3, 0)):
-            for d in (2, 1, 3):
-                send(block(s, d, k), xin.at[s, d - 1, n], e_sems.at[d - 1, n], dx=d)
+        for k in (1, 3, 2, 0):
+            for d in (2, 1, 3) if k != 2 else (2, 1, 3, 0):
+                if k == 2:
+                    send(block(s, d, k), oin.at[d], o_sems.at[d], dx=d, dyh=2)
+                else:
+                    n = (1, 3, 0).index(k)
+                    send(block(s, d, k), xin.at[s, d - 1, n], e_sems.at[d - 1, n], dx=d)
 
     def x_last_short(s):
         for n, k in enumerate((1, 3, 0)):
@@ -204,7 +213,7 @@
     pl.semaphore_wait(far, 2)
     for d in (2, 1, 3):
         signal(cross, at(dx=d))
-    for q in range(4):
+    for q in (0, 2, 1, 3):
         relay((0, 6), q, ((0, 5), up), ((1, 6), over))
         relay((0, 2), q, ((0, 3), down), ((1, 2), over))
         relay((1, 7), q, ((1, 5), dict(dz=2)))
@@ -212,7 +221,7 @@
     multiply(1)
     x_first(1)
     pl.semaphore_wait(cross, 3)
-    for q in (2, 0, 1, 3):
+    for q in (0, 2, 1, 3):
         relay((0, 4), q, ((1, 4), over))
     got((1, 2), (1, 6), (0, 3))
     multiply(2)

time: 59.9 us -> 60.2 us (level)
  no operation moved by 1% of the time
where the time goes in v5:
time: 60.2 us; the launch traced here: 60.1 us
  Pallas kernels  59.5 us (99%)
  local copies, waits for them, and re-layouts  0.63 us (1%)
    pallas_call x1, Pallas kernels, per_device(): pl.pallas_call(kernel, out_shape=jax.ShapeDtypeStruct((nrow, m), f32), in...  59.5 us

profile of v5, /device:TPU:1, one launch (start us, length us, event | category | flops | bytes accessed | tf_op | source)
XLA Modules:
  0.0 60.1 jit_solution(7505596369561611019)
XLA Ops:
  0.0 59.5 %shard_map.64 = f32[16,1000]{1,0:T(8,128)S(1)} custom-call(bf16[1000,256]{1,0:T(8,128)(2,1)} %bitcast.7, bf16[16,1000]{1,0:T(8,128)(2,1)} %bitcast.8, bf16[16,1000]{1,0:T(8,128)(2,1)} %bitcast.9, f32[1,256]{1,0:T(1,128)} %bitcast.10, s32[1,8]{1,0:T(1,128)} %bitcast.11, s32[8,8]{1,0:T(8,128)} %sig_hbm.1), custom_call_target="tpu_custom_call" | custom-call | tf_op jit(solution)/shard_map/pallas_call | solution.py:344
  59.5 0.6 %copy.8 = f32[1000,16]{0,1:T(8,128)} copy(f32[1000,16]{0,1:T(8,128)S(1)} %bitcast.6) | data formatting | bytes 128000

commit v6 on v5

--- a/solution.py
+++ b/solution.py
@@ -18,6 +18,7 @@
     ((0, 4), (0, 3), (1, 2), (1, 6)),
     ((0, 5), (1, 4), (1, 3), (1, 5)),
 )
+RELAYED = ((0, 7), (0, 1), (0, 6), (0, 2), (1, 7), (1, 1), (0, 4))
 WHERE = {slot: (s, i) for s, row in enumerate(SETS) for i, slot in enumerate(row)}
 
 
@@ -27,7 +28,7 @@
     xin, oin,
     turned, yrecv, dens_out, dens_in, kall,
     xsend, xrecv, zsend, zrecv,
-    sems, p_sems, c_sems, x_sems, e_sems, o_sems, y_sems, k_sems, d_sems, l_sems,
+    sems, p_sems, g_sems, c_sems, x_sems, e_sems, o_sems, y_sems, k_sems, d_sems, l_sems,
     near, far, ready_x, ready_z, far_z, cross,
 ):
     g, o = lax.axis_index("grid"), lax.axis_index("occ")
@@ -42,15 +43,21 @@
     def occ_at(dx, dyh):
         return ((x + dx) % NX) * NYH + (yh + dyh) % NYH
 
-    sent = []
-
-    def send(src, dst, recv_sem, dy=0, dz=0, dc=0, dx=0, dyh=0):
-        copy = pltpu.make_async_remote_copy(
-            src_ref=src, dst_ref=dst, send_sem=sems.at[len(sent)], recv_sem=recv_sem,
-            device_id=at(dy, dz, dc, dx, dyh), device_id_type=MESH,
-        )
-        copy.start()
-        sent.append(copy)
+    amount = {}
+
+    def send(src, dst, recv_sem, group, **where):
+        pltpu.make_async_remote_copy(
+            src_ref=src, dst_ref=dst, send_sem=sems.at[group], recv_sem=recv_sem,
+            device_id=at(**where), device_id_type=MESH,
+        ).start()
+        amount[group] = amount.get(group, 0) + math.prod(src.shape) * src.dtype.itemsize
+
+    def all_sent(group, ref):
+        assert amount[group] == math.prod(ref.shape) * ref.dtype.itemsize
+        pltpu.make_async_remote_copy(
+            src_ref=ref, dst_ref=ref, send_sem=sems.at[group], recv_sem=sems.at[group],
+            device_id=at(dc=1), device_id_type=MESH,
+        ).wait_send()
 
     def arrive(dst, recv_sem):
         pltpu.make_async_remote_copy(
@@ -94,12 +101,12 @@
 
     def p_sem(slot, q):
         s, i = WHERE[slot]
-        return p_sems.at[(s * 4 + i) * 4 + q]
+        return p_sems.at[RELAYED.index(slot) * 4 + q] if slot in RELAYED else g_sems.at[s * 4 + i]
 
     def leave(own, q):
-        send(own, place((0, 7), q), p_sem((0, 7), q), dz=1)
-        send(own, place((0, 1), q), p_sem((0, 1), q), dz=7)
-        send(own, place((1, 0), q), p_sem((1, 0), q), dy=1)
+        send(own, place((0, 7), q), p_sem((0, 7), q), 1, dz=1)
+        send(own, place((0, 1), q), p_sem((0, 1), q), 1, dz=7)
+        send(own, place((1, 0), q), p_sem((1, 0), q), 1, dy=1)
 
     leave(occ_hbm.at[:, pl.ds(0, wide // 2)], 0)
     leave(tri_hbm.at[:, pl.ds(0, wide // 2)], 2)
@@ -109,21 +116,21 @@
     panels[0, :, 0, :, m:] = jnp.zeros((2, nrow, wide - m), panels.dtype)
     for q in (1, 3):
         leave(place((0, 0), q), q)
-    send(sig_hbm, sigp, c_sems.at[0], dc=1)
-    send(v_hbm, vraw, c_sems.at[1], dc=1)
+    send(sig_hbm, sigp, c_sems.at[0], 2, dc=1)
+    send(v_hbm, vraw, c_sems.at[1], 3, dc=1)
     pl.semaphore_wait(ready_z, 2)
     for step in (2, 6):
         signal(far_z, at(dz=step))
 
     def got(*slots):
         for slot in slots:
-            for q in range(4):
-                arrive(place(slot, q), p_sem(slot, q))
+            s, i = WHERE[slot]
+            arrive(panels.at[s, :, i], p_sem(slot, 0))
 
     def relay(slot, q, *moves):
         arrive(place(slot, q), p_sem(slot, q))
         for to, step in moves:
-            send(place(slot, q), place(to, q), p_sem(to, q), **step)
+            send(place(slot, q), place(to, q), p_sem(to, q), 0, **step)
 
     up, down, over = dict(dz=1), dict(dz=7), dict(dy=1)
 
@@ -180,31 +187,29 @@
 
     def x_first(s):
         for d in (2, 1, 3):
-            send(prod.at[s, (x + d) % NX], xin.at[s, d - 1], x_sems.at[s, d - 1], dx=d)
+            send(prod.at[s, (x + d) % NX], xin.at[s, d - 1], x_sems.at[s], 4, dx=d)
 
     def x_last(s):
-        for d in range(1, NX):
-            arrive(xin.at[s, d - 1], x_sems.at[s, d - 1])
+        arrive(xin.at[s], x_sems.at[s])
         turned[s] = prod[s, x] + xin[s, 0] + xin[s, 1] + xin[s, 2]
         for k in (2, 1, 3):
-            send(turned.at[s, (yh + k) % NYH], yrecv.at[s, k - 1], y_sems.at[s, k - 1], dyh=k)
+            send(turned.at[s, (yh + k) % NYH], yrecv.at[s, k - 1], y_sems.at[s], 5, dyh=k)
 
     def x_first_short(s):
         for k in (1, 3, 2, 0):
             for d in (2, 1, 3) if k != 2 else (2, 1, 3, 0):
                 if k == 2:
-                    send(block(s, d, k), oin.at[d], o_sems.at[d], dx=d, dyh=2)
+                    send(block(s, d, k), oin.at[d], o_sems.at[0], 6, dx=d, dyh=2)
                 else:
                     n = (1, 3, 0).index(k)
-                    send(block(s, d, k), xin.at[s, d - 1, n], e_sems.at[d - 1, n], dx=d)
+                    send(block(s, d, k), xin.at[s, d - 1, n], e_sems.at[n], 7, dx=d)
 
     def x_last_short(s):
         for n, k in enumerate((1, 3, 0)):
-            for d in range(1, NX):
-                arrive(xin.at[s, d - 1, n], e_sems.at[d - 1, n])
+            arrive(xin.at[s, :, n], e_sems.at[n])
             turned[s, n] = prod[s, x, (yh + k) % NYH] + xin[s, 0, n] + xin[s, 1, n] + xin[s, 2, n]
             if k:
-                send(turned.at[s, n], yrecv.at[s, k - 1], y_sems.at[s, k - 1], dyh=k)
+                send(turned.at[s, n], yrecv.at[s, n], y_sems.at[s], 8, dyh=k)
 
     got((1, 0))
     pl.semaphore_wait(ready_x, 2)
@@ -239,14 +244,14 @@
     part = jnp.zeros((CAP, 1), jnp.float32)
     for s in range(4):
         unit = turned[s, yh] if s < 3 else turned[s, 2]
-        for k in (1, 2, 3):
-            if s < 3 or k != 2:
-                arrive(yrecv.at[s, k - 1], y_sems.at[s, k - 1])
-                unit = unit + yrecv[s, k - 1]
-            else:
-                for d in range(NX):
-                    arrive(oin.at[d], o_sems.at[d])
-                    unit = unit + oin[d]
+        if s < 3:
+            arrive(yrecv.at[s], y_sems.at[s])
+            unit = unit + yrecv[s, 0] + yrecv[s, 1] + yrecv[s, 2]
+        else:
+            arrive(oin, o_sems.at[0])
+            unit = unit + oin[0] + oin[1] + oin[2] + oin[3]
+            arrive(yrecv.at[s, pl.ds(0, 2)], y_sems.at[s])
+            unit = unit + yrecv[s, 0] + yrecv[s, 1]
         other = pltpu.roll(unit, half, 1)
         units.append(unit)
         rolled.append(other)
@@ -268,7 +273,7 @@
     live = lax.broadcasted_iota(jnp.int32, (CAP, 1), 0).astype(jnp.float32) < count
     weight = jnp.where(live, weight, 0.0)
     dens_out[...] = jnp.where(lane < half, part, weight)
-    send(dens_out, dens_in, d_sems.at[0], dc=1)
+    send(dens_out, dens_in, d_sems.at[0], 9, dc=1)
     arrive(dens_in, d_sems.at[0])
     total = 2 * nrow * NYL * NZ
     density = (part + dens_in[:, 0:1]) * (1.0 / math.sqrt(total))
@@ -285,18 +290,16 @@
 
     for p in (1, 0):
         for k in (2, 1, 3):
-            send(k_from(p, 0, 0), k_from(p, 0, 0), k_sems.at[p, 0, NYH - k], dyh=k)
+            send(k_from(p, 0, 0), k_from(p, 0, 0), k_sems.at[p, NYH - k], 10, dyh=k)
     for p in (1, 0):
         for k in (0, 1, 3, 2):
             if k:
-                arrive(k_from(p, 0, k), k_sems.at[p, 0, k])
+                arrive(k_from(p, 0, k), k_sems.at[p, k])
             for d in (2, 1, 3):
-                send(k_from(p, 0, k), k_from(p, 0, k), k_sems.at[p, NX - d, k], dx=d)
+                send(k_from(p, 0, k), k_from(p, 0, k), k_sems.at[p, 0], 10, dx=d)
     held = {}
     for p in (1, 0):
-        for k in (0, 1, 3, 2):
-            for d in (1, 3, 2):
-                arrive(k_from(p, d, k), k_sems.at[p, d, k])
+        arrive(kall.at[p, pl.ds(0, (NX - 1) * NYH)], k_sems.at[p, 0])
         kt = kall[p].reshape(2 * npt, 2 * half).T
         res = sum(
             jnp.dot(
@@ -312,7 +315,7 @@
                     block = res[i * nrow : (i + 1) * nrow]
                     if dy:
                         xsend[dz] = block.astype(jnp.bfloat16)
-                        send(xsend.at[dz], xrecv.at[dz], d_sems.at[1 + dz], dy=1)
+                        send(xsend.at[dz], xrecv.at[dz], d_sems.at[1 + dz], 11, dy=1)
                     else:
                         held[dz] = block
     mine = None
@@ -321,11 +324,15 @@
         value = held[dz] + xrecv[dz].astype(jnp.float32)
         if dz:
             zsend[dz - 1] = value.astype(jnp.bfloat16)
-            send(zsend.at[dz - 1], zrecv.at[dz - 1], d_sems.at[8 + dz], dz=dz)
+            send(zsend.at[dz - 1], zrecv.at[dz - 1], d_sems.at[8 + dz], 12, dz=dz)
         else:
             mine = value
-    for copy in sent:
-        copy.wait_send()
+    for group, ref in enumerate((
+        panels.at[pl.ds(0, 3)], panels.at[0, :, pl.ds(0, 3)], sigp, vraw, xin.at[pl.ds(0, 3)],
+        yrecv.at[pl.ds(0, 3)], oin, xin.at[3, :, pl.ds(0, 3)], yrecv.at[3, pl.ds(0, 2)], dens_in,
+        kall.at[:, pl.ds(0, 15)], xsend, zsend,
+    )):
+        all_sent(group, ref)
     for dz in (1, 7, 2, 6, 3, 5, 4):
         arrive(zrecv.at[dz - 1], d_sems.at[8 + dz])
         mine = mine + zrecv[dz - 1].astype(jnp.float32)
@@ -370,14 +377,15 @@
             pltpu.VMEM((NZ, nrow, wide), bf16),
             pltpu.VMEM((NZ - 1, nrow, wide), bf16),
             pltpu.VMEM((NZ - 1, nrow, wide), bf16),
-            dma((192,)),
-            dma((64,)),
+            dma((13,)),
+            dma((28,)),
+            dma((16,)),
             dma((2,)),
-            dma((3, NX - 1)),
-            dma((NX - 1, 3)),
-            dma((NX,)),
-            dma((4, NYH - 1)),
-            dma((2, NX, NYH)),
+            dma((3,)),
+            dma((3,)),
+            dma((1,)),
+            dma((4,)),
+            dma((2, NYH)),
             dma((1 + 8 + 8,)),
             dma((6,)),
         ]

time: 60.2 us -> 58 us (0.963)
  Pallas kernels: 59.5 us -> 57.3 us
    pallas_call x1, Pallas kernels: 59.5 us -> 57.3 us  [per_device(): pl.pallas_call(kernel, out_shape=jax.ShapeDtypeStruct((nrow, m), f32), in...]
where the time goes in v6:
time: 58 us; the launch traced here: 57.9 us
  Pallas kernels  57.3 us (99%)
  local copies, waits for them, and re-layouts  0.63 us (1%)
    pallas_call x1, Pallas kernels, per_device(): pl.pallas_call(kernel, out_shape=jax.ShapeDtypeStruct((nrow, m), f32), in...  57.3 us

profile of v6, /device:TPU:1, one launch (start us, length us, event | category | flops | bytes accessed | tf_op | source)
XLA Modules:
  0.0 57.9 jit_solution(15294223795865465613)
XLA Ops:
  0.0 57.3 %shard_map.64 = f32[16,1000]{1,0:T(8,128)S(1)} custom-call(bf16[1000,256]{1,0:T(8,128)(2,1)} %bitcast.7, bf16[16,1000]{1,0:T(8,128)(2,1)} %bitcast.8, bf16[16,1000]{1,0:T(8,128)(2,1)} %bitcast.9, f32[1,256]{1,0:T(1,128)} %bitcast.10, s32[1,8]{1,0:T(1,128)} %bitcast.11, s32[8,8]{1,0:T(8,128)} %sig_hbm.1), custom_call_target="tpu_custom_call" | custom-call | tf_op jit(solution)/shard_map/pallas_call | solution.py:351
  57.3 0.6 %copy.8 = f32[1000,16]{0,1:T(8,128)} copy(f32[1000,16]{0,1:T(8,128)S(1)} %bitcast.6) | data formatting | bytes 128000

commit v7 on v6

--- a/solution.py
+++ b/solution.py
@@ -19,6 +19,7 @@
     ((0, 5), (1, 4), (1, 3), (1, 5)),
 )
 RELAYED = ((0, 7), (0, 1), (0, 6), (0, 2), (1, 7), (1, 1), (0, 4))
+GOT = ((1, 0), (1, 2), (1, 6), (0, 3), (0, 5), (1, 4), (1, 3), (1, 5))
 WHERE = {slot: (s, i) for s, row in enumerate(SETS) for i, slot in enumerate(row)}
 
 
@@ -101,7 +102,7 @@
 
     def p_sem(slot, q):
         s, i = WHERE[slot]
-        return p_sems.at[RELAYED.index(slot) * 4 + q] if slot in RELAYED else g_sems.at[s * 4 + i]
+        return p_sems.at[RELAYED.index(slot) * 4 + q] if slot in RELAYED else g_sems.at[GOT.index(slot)]
 
     def leave(own, q):
         send(own, place((0, 7), q), p_sem((0, 7), q), 1, dz=1)
@@ -235,6 +236,21 @@
     got((0, 5), (1, 4), (1, 5), (1, 3))
     multiply(3)
     x_first_short(3)
+    batch = o % nbatch
+    row_of = lax.broadcasted_iota(jnp.int32, (CAP, npt), 0)
+    lane_of = lax.broadcasted_iota(jnp.int32, (CAP, npt), 1)
+    weight = jnp.sum(
+        jnp.where(lane_of == row_of + batch * CAP, w_ref[...], 0.0), axis=1, keepdims=True
+    )
+    count = jnp.sum(
+        jnp.where(
+            lax.broadcasted_iota(jnp.int32, (1, nbatch), 1) == batch,
+            sz_ref[...].astype(jnp.float32), 0.0,
+        ),
+        axis=1, keepdims=True,
+    )
+    live = lax.broadcasted_iota(jnp.int32, (CAP, 1), 0).astype(jnp.float32) < count
+    weight = jnp.where(live, weight, 0.0)
     x_last(1)
     x_last(2)
     x_last_short(3)
@@ -257,21 +273,6 @@
         rolled.append(other)
         part += jnp.sum(jnp.where(lane < half, unit * other, 0.0), axis=1, keepdims=True)
 
-    batch = o % nbatch
-    row_of = lax.broadcasted_iota(jnp.int32, (CAP, npt), 0)
-    lane_of = lax.broadcasted_iota(jnp.int32, (CAP, npt), 1)
-    weight = jnp.sum(
-        jnp.where(lane_of == row_of + batch * CAP, w_ref[...], 0.0), axis=1, keepdims=True
-    )
-    count = jnp.sum(
-        jnp.where(
-            lax.broadcasted_iota(jnp.int32, (1, nbatch), 1) == batch,
-            sz_ref[...].astype(jnp.float32), 0.0,
-        ),
-        axis=1, keepdims=True,
-    )
-    live = lax.broadcasted_iota(jnp.int32, (CAP, 1), 0).astype(jnp.float32) < count
-    weight = jnp.where(live, weight, 0.0)
     dens_out[...] = jnp.where(lane < half, part, weight)
     send(dens_out, dens_in, d_sems.at[0], 9, dc=1)
     arrive(dens_in, d_sems.at[0])
@@ -324,7 +325,7 @@
         value = held[dz] + xrecv[dz].astype(jnp.float32)
         if dz:
             zsend[dz - 1] = value.astype(jnp.bfloat16)
-            send(zsend.at[dz - 1], zrecv.at[dz - 1], d_sems.at[8 + dz], 12, dz=dz)
+            send(zsend.at[dz - 1], zrecv.at[dz - 1], d_sems.at[9], 12, dz=dz)
         else:
             mine = value
     for group, ref in enumerate((
@@ -333,8 +334,8 @@
         kall.at[:, pl.ds(0, 15)], xsend, zsend,
     )):
         all_sent(group, ref)
-    for dz in (1, 7, 2, 6, 3, 5, 4):
-        arrive(zrecv.at[dz - 1], d_sems.at[8 + dz])
+    arrive(zrecv, d_sems.at[9])
+    for dz in range(1, NZ):
         mine = mine + zrecv[dz - 1].astype(jnp.float32)
     points = npt * NYL * NZ * NC
     out_ref[...] = mine[:, :m] * (1.0 / math.sqrt(points))
@@ -379,14 +380,14 @@
             pltpu.VMEM((NZ - 1, nrow, wide), bf16),
             dma((13,)),
             dma((28,)),
-            dma((16,)),
+            dma((8,)),
             dma((2,)),
             dma((3,)),
             dma((3,)),
             dma((1,)),
             dma((4,)),
             dma((2, NYH)),
-            dma((1 + 8 + 8,)),
+            dma((1 + 8 + 1,)),
             dma((6,)),
         ]
         + [pltpu.SemaphoreType.REGULAR] * 6,

time: 58 us -> 57.8 us (level)
  no operation moved by 1% of the time
where the time goes in v7:
time: 57.8 us; the launch traced here: 57.7 us
  Pallas kernels  57.1 us (99%)
  local copies, waits for them, and re-layouts  0.63 us (1%)
    pallas_call x1, Pallas kernels, per_device(): pl.pallas_call(kernel, out_shape=jax.ShapeDtypeStruct((nrow, m), f32), in...  57.1 us

profile of v7, /device:TPU:1, one launch (start us, length us, event | category | flops | bytes accessed | tf_op | source)
XLA Modules:
  0.0 57.7 jit_solution(13002277263872489415)
XLA Ops:
  0.0 57.1 %shard_map.64 = f32[16,1000]{1,0:T(8,128)S(1)} custom-call(bf16[1000,256]{1,0:T(8,128)(2,1)} %bitcast.7, bf16[16,1000]{1,0:T(8,128)(2,1)} %bitcast.8, bf16[16,1000]{1,0:T(8,128)(2,1)} %bitcast.9, f32[1,256]{1,0:T(1,128)} %bitcast.10, s32[1,8]{1,0:T(1,128)} %bitcast.11, s32[8,8]{1,0:T(8,128)} %sig_hbm.1), custom_call_target="tpu_custom_call" | custom-call | tf_op jit(solution)/shard_map/pallas_call | solution.py:352
  57.1 0.6 %copy.8 = f32[1000,16]{0,1:T(8,128)} copy(f32[1000,16]{0,1:T(8,128)S(1)} %bitcast.6) | data formatting | bytes 128000
